TPU v7x, 32 devices: a whole 2x2x4 slice. The times are simulated.
32 devices in a mesh: groups: 2 (over x), dp: 16 (over z, y, core).
Axes of the slice: x: 2, y: 2, z: 4, core: 2. Of those that a mesh axis runs over, the one named last changes fastest.
Arguments:
- tokens: bfloat16 [24576, 1024], P(('groups', 'dp')), parts along dimension 0, may hold values from -6 to 6
- token_mask: int32 [32, 768], P(('groups', 'dp')), parts along dimension 0, may hold values 0 or 1
- span_ids: int32 [32, 768], P(('groups', 'dp')), parts along dimension 0, may hold values from 0 to 191, never falling along the last dimension, each value on 1 to 8 neighbouring positions
- norm_gain: float32 [1024], replicated, may hold values from 0.1 to 1.9
- norm_shift: float32 [1024], replicated, may hold values from -3 to 3
- w_up: bfloat16 [1024, 4096], P(None, 'dp'), may hold values from -0.1875 to 0.1875
- b_up: float32 [4096], replicated, may hold values from -3 to 3
- w_down: bfloat16 [4096, 1024], P(None, 'dp'), may hold values from -0.09375 to 0.09375
Outputs:
- whitened: float32 [6144, 1024], P(('groups', 'dp')), parts along dimension 0
There are 2 independent parts, one for each index of `groups`. A program takes and returns all parts, laid end to end along the dimension named above; an argument that names none is the same for every part. Nothing has to cross between parts.
Inputs may be any that keep to these rules, and one draw needn't show every extreme that they name: `span_ids`: in each row the span numbers never fall, every span 0 to 191 holds 1 to 8 tokens, and one holds exactly 8.
All inputs are finite; a program needn't handle non-finite values. No bound on the sum of `token_mask` on one device may be relied on, other than what follows from the above.
Results may differ from a plain program's by a relative error of at most 0.0095.
Values may be sent and summed in bfloat16 or wider, within the bound.
A program may use at most 128 MiB of HBM per device.

v0:
```python
import math
import jax
import jax.numpy as jnp
from jax import lax
from jax.sharding import PartitionSpec as P

SEG_DEV = 192


def on_device(tokens, token_mask, span_ids, norm_gain, norm_shift, w_up, b_up, w_down):
    values = tokens.astype(jnp.float32)
    center = jnp.mean(values, axis=1, keepdims=True)
    spread = jnp.mean((values - center) ** 2, axis=1, keepdims=True)
    normed = ((values - center) * lax.rsqrt(spread + 1e-05) * norm_gain + norm_shift).astype(
        jnp.bfloat16
    )
    up_full, down_full = (
        lax.all_gather(w_up, "dp", axis=1, tiled=True),
        lax.all_gather(w_down, "dp", axis=1, tiled=True),
    )
    before = jnp.dot(normed, up_full, preferred_element_type=jnp.float32) + b_up
    hidden = jax.nn.gelu(before, approximate=False).astype(jnp.bfloat16)
    projected = jnp.dot(hidden, down_full, preferred_element_type=jnp.float32)
    block_out = (values + projected).astype(jnp.bfloat16)
    labels = jnp.arange(SEG_DEV, dtype=jnp.int32)[:, None]
    select = (span_ids[0][None, :] == labels) & (token_mask[0][None, :] == 1)
    sums = jnp.dot(select.astype(jnp.bfloat16), block_out, preferred_element_type=jnp.float32)
    counts = jnp.sum(select.astype(jnp.float32), axis=1)
    pooled = (sums / jnp.maximum(counts, 1.0)[:, None]).astype(jnp.bfloat16)
    partial_gram = jnp.dot(pooled.T, pooled, preferred_element_type=jnp.float32)
    gram = lax.psum(partial_gram, "dp")
    lower = jnp.linalg.cholesky(gram)
    solved = jax.scipy.linalg.solve_triangular(lower, pooled.astype(jnp.float32).T, lower=True)
    total_rows = SEG_DEV * lax.axis_size("dp")
    return math.sqrt(total_rows) * solved.T


def solution(mesh):
    in_specs = (
        P(("groups", "dp"), None),
        P(("groups", "dp"), None),
        P(("groups", "dp"), None),
        P(),
        P(),
        P(None, "dp"),
        P(),
        P(None, "dp"),
    )
    out_specs = P(("groups", "dp"), None)
    return jax.shard_map(
        on_device, mesh=mesh, in_specs=in_specs, out_specs=out_specs, check_vma=False
    )
```

profile of v0, /device:TPU:0, one launch (start us, length us, event | category | flops | bytes accessed | tf_op | source)
XLA Modules:
  0.0 630.8 jit_solution(12674228877443732165)
XLA Ops:
  13.3 77.0 %all-gather.3.cloned.1.call-done = bf16[1024,4096]{1,0:T(8,128)(2,1)} async-done(((bf16[1024,256]{1,0:T(8,128)(2,1)}), bf16[1024,4096]{1,0:T(8,128)(2,1)}) %all-gather.3.cloned.1.call-update) | async-done | bytes 8388624 | tf_op jit(solution)/shard_map/all_gather | solution.py:18
  90.4 37.2 %fusion.2.clone.6 = bf16[768,4096]{1,0:T(8,128)(2,1)} fusion(bf16[1024,4096]{1,0:T(8,128)(2,1)} %all-gather.3.cloned.1.call-done, f32[4096]{0:T(1024)S(1)} %copy-done.2, bf16[768,1024]{1,0:T(8,128)(2,1)S(1)} %copy-done.1, f32[1024]{0:T(1024)S(1)} %copy-done.3, f32[1024]{0:T(1024)S(1)} %copy-done.4, ...), kind=kOutput, calls=%fused_computation.5.clone.clone.clone.clone.clone.1 | convolution fusion | flops 6654787584 | bytes 16283648 | tf_op jit(solution)/shard_map/dot_general | solution.py:21
  127.5 38.1 %all-gather.5.cloned.1.call-done = bf16[4096,1024]{0,1:T(8,128)(2,1)} async-done(((bf16[4096,64]{0,1:T(8,128)(2,1)}), bf16[4096,1024]{0,1:T(8,128)(2,1)}) %all-gather.5.cloned.1.call-update) | async-done | bytes 8388624 | tf_op jit(solution)/shard_map/all_gather | solution.py:19
  165.6 11.2 %fusion.49 = bf16[768,1024]{1,0:T(8,128)(2,1)S(1)} fusion(bf16[768,1024]{1,0:T(8,128)(2,1)S(1)} %copy-done.1, bf16[4096,1024]{0,1:T(8,128)(2,1)} %all-gather.5.cloned.1.call-done, bf16[768,4096]{1,0:T(8,128)(2,1)} %fusion.2.clone.6), kind=kOutput, calls=%fused_computation.66 | convolution fusion | flops 6444810240 | bytes 17825792 | tf_op jit(solution)/shard_map/dot_general | solution.py:23
  180.0 109.8 %all-reduce.3.cloned.1.call-done = f32[1024,1024]{0,1:T(8,128)} async-done(((f32[1024,1024]{0,1:T(8,128)}), f32[1024,1024]{0,1:T(8,128)}) %all-reduce.3.cloned.1.call-update) | async-done | bytes 4194320 | tf_op jit(solution)/shard_map/psum | solution.py:31
  289.9 5.3 copy.12
  301.6 11.7 %cholesky.223 = f32[128,128]{1,0:T(8,128)S(1)} custom-call(f32[128,128]{1,0:T(8,128)S(1)} %cholesky.580), custom_call_target="Cholesky" | custom-call | tf_op jit(solution)/shard_map/jit(cholesky)/cholesky | solution.py:32
  313.3 9.8 %custom-call.63 = f32[1,128,128]{1,2,0:T(8,128)S(1)} custom-call(f32[1,128,128]{2,1,0:T(8,128)S(1)} %get-tuple-element.69), custom_call_target="InvertDiagBlocksLowerTriangular" | custom-call | tf_op jit(solution)/shard_map/jit(cholesky)/cholesky | solution.py:32
  329.6 12.1 %cholesky.244 = f32[128,128]{1,0:T(8,128)S(1)} custom-call(f32[128,128]{1,0:T(8,128)S(1)} %cholesky.584), custom_call_target="Cholesky" | custom-call | tf_op jit(solution)/shard_map/jit(cholesky)/cholesky | solution.py:32
  342.3 9.8 %custom-call.64 = f32[1,128,128]{1,2,0:T(8,128)S(1)} custom-call(f32[1,128,128]{2,1,0:T(8,128)S(1)} %get-tuple-element.66), custom_call_target="InvertDiagBlocksLowerTriangular" | custom-call | tf_op jit(solution)/shard_map/jit(cholesky)/cholesky | solution.py:32
  355.5 11.7 %cholesky.468 = f32[128,128]{1,0:T(8,128)S(1)} custom-call(f32[128,128]{1,0:T(8,128)S(1)} %cholesky.589), custom_call_target="Cholesky" | custom-call | tf_op jit(solution)/shard_map/jit(cholesky)/cholesky | solution.py:32
  368.5 9.8 %custom-call.65 = f32[1,128,128]{1,2,0:T(8,128)S(1)} custom-call(f32[1,128,128]{2,1,0:T(8,128)S(1)} %get-tuple-element.63), custom_call_target="InvertDiagBlocksLowerTriangular" | custom-call | tf_op jit(solution)/shard_map/jit(cholesky)/cholesky | solution.py:32
  381.8 11.8 %cholesky.487 = f32[128,128]{1,0:T(8,128)S(1)} custom-call(f32[128,128]{1,0:T(8,128)S(1)} %cholesky.594), custom_call_target="Cholesky" | custom-call | tf_op jit(solution)/shard_map/jit(cholesky)/cholesky | solution.py:32
  394.9 9.8 %custom-call.66 = f32[1,128,128]{1,2,0:T(8,128)S(1)} custom-call(f32[1,128,128]{2,1,0:T(8,128)S(1)} %get-tuple-element.60), custom_call_target="InvertDiagBlocksLowerTriangular" | custom-call | tf_op jit(solution)/shard_map/jit(cholesky)/cholesky | solution.py:32
  408.2 11.7 %cholesky.506 = f32[128,128]{1,0:T(8,128)S(1)} custom-call(f32[128,128]{1,0:T(8,128)S(1)} %cholesky.599), custom_call_target="Cholesky" | custom-call | tf_op jit(solution)/shard_map/jit(cholesky)/cholesky | solution.py:32
  421.2 10.0 %custom-call.67 = f32[1,128,128]{1,2,0:T(8,128)S(1)} custom-call(f32[1,128,128]{2,1,0:T(8,128)S(1)} %get-tuple-element.57), custom_call_target="InvertDiagBlocksLowerTriangular" | custom-call | tf_op jit(solution)/shard_map/jit(cholesky)/cholesky | solution.py:32
  434.5 11.7 %cholesky.526 = f32[128,128]{1,0:T(8,128)S(1)} custom-call(f32[128,128]{1,0:T(8,128)S(1)} %cholesky.604), custom_call_target="Cholesky" | custom-call | tf_op jit(solution)/shard_map/jit(cholesky)/cholesky | solution.py:32
  447.5 9.8 %custom-call.68 = f32[1,128,128]{1,2,0:T(8,128)S(1)} custom-call(f32[1,128,128]{2,1,0:T(8,128)S(1)} %get-tuple-element.54), custom_call_target="InvertDiagBlocksLowerTriangular" | custom-call | tf_op jit(solution)/shard_map/jit(cholesky)/cholesky | solution.py:32
  460.3 12.1 %cholesky.546 = f32[128,128]{1,0:T(8,128)S(1)} custom-call(f32[128,128]{1,0:T(8,128)S(1)} %cholesky.609), custom_call_target="Cholesky" | custom-call | tf_op jit(solution)/shard_map/jit(cholesky)/cholesky | solution.py:32
  473.6 9.8 %custom-call.69 = f32[1,128,128]{1,2,0:T(8,128)S(1)} custom-call(f32[1,128,128]{2,1,0:T(8,128)S(1)} %get-tuple-element.51), custom_call_target="InvertDiagBlocksLowerTriangular" | custom-call | tf_op jit(solution)/shard_map/jit(cholesky)/cholesky | solution.py:32
  486.1 11.7 %cholesky.564 = f32[128,128]{1,0:T(8,128)S(1)} custom-call(f32[128,128]{1,0:T(8,128)S(1)} %convolution_subtract_fusion.13), custom_call_target="Cholesky" | custom-call | tf_op jit(solution)/shard_map/jit(cholesky)/cholesky | solution.py:32
  504.6 4.8 select_select_fusion
  509.4 22.8 %while.1 = (s32[]{:T(128)}, f32[1024,1024]{1,0:T(8,128)}, s32[8,2]{0,1:T(2,128)S(1)}, f32[8,128,128]{2,1,0:T(8,128)S(1)}, s32[]{:T(128)}) while((s32[]{:T(128)}, f32[1024,1024]{1,0:T(8,128)}, s32[8,2]{0,1:T(2,128)S(1)}, f32[8,128,128]{2,1,0:T(8,128)S(1)}, s32[]{:T(128)}) %tuple.58), condition=%wide.while_cond, body=%wide.while_body.sunk | while | flops 2 | bytes 131181 | solution.py:33
  532.3 78.8 %custom-call.70 = f32[8,128,128]{1,2,0:T(8,128)S(1)} custom-call(f32[8,128,128]{2,1,0:T(8,128)S(1)} %get-tuple-element.12), custom_call_target="InvertDiagBlocksLowerTriangular" | custom-call | tf_op jit(solution)/shard_map/jit(_solve_triangular)/triangular_solve | solution.py:33
  (107 shorter events, 86.6 us)
Async XLA Ops:
  6.5 83.8 %copy-start.1 = (bf16[768,1024]{1,0:T(8,128)(2,1)S(1)}, bf16[768,1024]{1,0:T(8,128)(2,1)}, u32[]{:S(2)}) copy-start(bf16[768,1024]{1,0:T(8,128)(2,1)} %param.8) | copy-start | bytes 4718596
  6.5 83.8 %copy-start.4 = (f32[1024]{0:T(1024)S(1)}, f32[1024]{0:T(1024)}, u32[]{:S(2)}) copy-start(f32[1024]{0:T(1024)} %param.11) | copy-start | bytes 12292
  6.5 83.8 %copy-start.3 = (f32[1024]{0:T(1024)S(1)}, f32[1024]{0:T(1024)}, u32[]{:S(2)}) copy-start(f32[1024]{0:T(1024)} %param.12) | copy-start | bytes 12292
  6.5 83.8 %copy-start.2 = (f32[4096]{0:T(1024)S(1)}, f32[4096]{0:T(1024)}, u32[]{:S(2)}) copy-start(f32[4096]{0:T(1024)} %param.14) | copy-start | bytes 49156
  6.5 83.8 %all-gather.3.cloned.1.call-start = ((), (), s32[]{:S(2)}) async-start(), calls=%async_computation | async-start | bytes 8912896 | tf_op jit(solution)/shard_map/all_gather | solution.py:18
  7.3 158.3 %all-gather.5.cloned.1.call-start = ((), (), s32[]{:S(2)}) async-start(), calls=%async_computation.1 | async-start | bytes 8912896 | tf_op jit(solution)/shard_map/all_gather | solution.py:19
  8.0 281.9 %all-reduce.3.cloned.1.call-start = ((), (), s32[]{:S(2)}) async-start(), calls=%async_computation.2 | async-start | bytes 8388608 | tf_op jit(solution)/shard_map/psum | solution.py:31
  299.7 1.9 copy-start
Sparse Core Ops, SparseCore 0:
  9.5 80.7 all-gather.2
  92.5 73.0 all-gather.4
  180.1 109.6 all-reduce.2
where the time goes:
time: 641 us; the launch traced here: 631 us
  other arithmetic  267 us (42%)
  waiting for transfers between devices  226 us (35%)
  matrix products  86.6 us (14%)
  local copies, waits for them, and re-layouts  32.5 us (5%)
  between operations  18.5 us (3%)
    another operation x30, other arithmetic, on_device(): lower = jnp.linalg.cholesky(gram)  172 us
    psum x1, waiting for transfers between devices, on_device(): gram = lax.psum(partial_gram, 'dp')  110 us
    another operation x3, other arithmetic, on_device(): jax.scipy.linalg.solve_triangular(lower, pooled.astype(jnp.float32).T, lo...  83.6 us
    all_gather x1, waiting for transfers between devices, on_device(): lax.all_gather(w_up, 'dp', axis=1, tiled=True)  77 us
    all_gather x1, waiting for transfers between devices, on_device(): lax.all_gather(w_down, 'dp', axis=1, tiled=True)  38.1 us
    dot_general x1, matrix products, on_device(): before = jnp.dot(normed, up_full, preferred_element_type=jnp.float32) + b_up  37.2 us
    another operation x14, matrix products, on_device(): lower = jnp.linalg.cholesky(gram)  23.1 us
    another operation x24, local copies, waits for them, and re-layouts  22.7 us
  transfers between devices with their start and end apart: 3, of which 3 were waited for; matrix products, arithmetic and copies ran while one was open for 7% of the time, Pallas kernels for 0%

commit v1 on v0

--- a/solution.py
+++ b/solution.py
@@ -28,7 +28,7 @@
     counts = jnp.sum(select.astype(jnp.float32), axis=1)
     pooled = (sums / jnp.maximum(counts, 1.0)[:, None]).astype(jnp.bfloat16)
     partial_gram = jnp.dot(pooled.T, pooled, preferred_element_type=jnp.float32)
-    gram = lax.psum(partial_gram, "dp")
+    gram = jnp.sum(lax.all_gather(partial_gram, "dp"), axis=0)
     lower = jnp.linalg.cholesky(gram)
     solved = jax.scipy.linalg.solve_triangular(lower, pooled.astype(jnp.float32).T, lower=True)
     total_rows = SEG_DEV * lax.axis_size("dp")

time: 641 us -> 879 us (1.37)
  waiting for transfers between devices: 226 us -> 441 us
  other arithmetic: 267 us -> 290 us
    all_gather x0 -> x1, waiting for transfers between devices: none -> 325 us  [on_device(): gram = jnp.sum(lax.all_gather(partial_gram, 'dp'), axis=0)]
    psum x1 -> x0, waiting for transfers between devices: 110 us -> none  [on_device(): gram = lax.psum(partial_gram, 'dp')]
    reduce_sum x0 -> x1, other arithmetic: none -> 22.9 us  [on_device(): gram = jnp.sum(lax.all_gather(partial_gram, 'dp'), axis=0)]
  transfers between devices with their start and end apart: 3 -> 3, of which waited for: 3 -> 3; matrix products, arithmetic and copies ran while one was open for 7% -> 5% of each run, Pallas kernels for 0% -> 0%
where the time goes in v1:
time: 879 us; the launch traced here: 868 us
  waiting for transfers between devices  441 us (50%)
  other arithmetic  290 us (33%)
  matrix products  86.6 us (10%)
  local copies, waits for them, and re-layouts  32.5 us (4%)
  between operations  18.5 us (2%)
    all_gather x1, waiting for transfers between devices, on_device(): gram = jnp.sum(lax.all_gather(partial_gram, 'dp'), axis=0)  325 us
    another operation x30, other arithmetic, on_device(): lower = jnp.linalg.cholesky(gram)  172 us
    another operation x3, other arithmetic, on_device(): jax.scipy.linalg.solve_triangular(lower, pooled.astype(jnp.float32).T, lo...  83.6 us
    all_gather x1, waiting for transfers between devices, on_device(): lax.all_gather(w_up, 'dp', axis=1, tiled=True)  77 us
    all_gather x1, waiting for transfers between devices, on_device(): lax.all_gather(w_down, 'dp', axis=1, tiled=True)  38.1 us
    dot_general x1, matrix products, on_device(): before = jnp.dot(normed, up_full, preferred_element_type=jnp.float32) + b_up  37.2 us
    another operation x14, matrix products, on_device(): lower = jnp.linalg.cholesky(gram)  23.1 us
    reduce_sum x1, other arithmetic, on_device(): gram = jnp.sum(lax.all_gather(partial_gram, 'dp'), axis=0)  22.9 us
  transfers between devices with their start and end apart: 3, of which 3 were waited for; matrix products, arithmetic and copies ran while one was open for 5% of the time, Pallas kernels for 0%

profile of v1, /device:TPU:0, one launch (start us, length us, event | category | flops | bytes accessed | tf_op | source)
XLA Modules:
  0.0 868.4 jit_solution(10103437613515064745)
XLA Ops:
  13.3 77.0 %all-gather.5.cloned.1.call-done = bf16[1024,4096]{1,0:T(8,128)(2,1)} async-done(((bf16[1024,256]{1,0:T(8,128)(2,1)}), bf16[1024,4096]{1,0:T(8,128)(2,1)}) %all-gather.5.cloned.1.call-update) | async-done | bytes 8388624 | tf_op jit(solution)/shard_map/all_gather | solution.py:18
  90.4 37.2 %fusion.2.clone.6 = bf16[768,4096]{1,0:T(8,128)(2,1)} fusion(bf16[1024,4096]{1,0:T(8,128)(2,1)} %all-gather.5.cloned.1.call-done, f32[4096]{0:T(1024)S(1)} %copy-done.2, bf16[768,1024]{1,0:T(8,128)(2,1)S(1)} %copy-done.1, f32[1024]{0:T(1024)S(1)} %copy-done.3, f32[1024]{0:T(1024)S(1)} %copy-done.4, ...), kind=kOutput, calls=%fused_computation.5.clone.clone.clone.clone.clone.1 | convolution fusion | flops 6654787584 | bytes 16283648 | tf_op jit(solution)/shard_map/dot_general | solution.py:21
  127.5 38.1 %all-gather.7.cloned.1.call-done = bf16[4096,1024]{0,1:T(8,128)(2,1)} async-done(((bf16[4096,64]{0,1:T(8,128)(2,1)}), bf16[4096,1024]{0,1:T(8,128)(2,1)}) %all-gather.7.cloned.1.call-update) | async-done | bytes 8388624 | tf_op jit(solution)/shard_map/all_gather | solution.py:19
  165.6 11.2 %fusion.49 = bf16[768,1024]{1,0:T(8,128)(2,1)S(1)} fusion(bf16[768,1024]{1,0:T(8,128)(2,1)S(1)} %copy-done.1, bf16[4096,1024]{0,1:T(8,128)(2,1)} %all-gather.7.cloned.1.call-done, bf16[768,4096]{1,0:T(8,128)(2,1)} %fusion.2.clone.6), kind=kOutput, calls=%fused_computation.66 | convolution fusion | flops 6444810240 | bytes 17825792 | tf_op jit(solution)/shard_map/dot_general | solution.py:23
  180.0 324.5 %all-gather.9.cloned.1.call-done = f32[16384,1024]{1,0:T(8,128)} async-done(((f32[1024,1024]{1,0:T(8,128)}), f32[16384,1024]{1,0:T(8,128)}) %all-gather.9.cloned.1.call-update) | async-done | bytes 67108880 | tf_op jit(solution)/shard_map/all_gather | solution.py:31
  504.6 22.9 %reduce_sum.39 = f32[1024,1024]{1,0:T(8,128)} reduce(f32[16,1024,1024]{2,1,0:T(8,128)} %bitcast, f32[]{:T(128)} %constant.305.clone.1), dimensions={0}, to_apply=%region_3.0 | reduce | flops 15728640 | bytes 71303168 | tf_op jit(solution)/shard_map/reduce_sum | solution.py:31
  527.5 5.3 copy.11
  539.2 11.7 %cholesky.223 = f32[128,128]{1,0:T(8,128)S(1)} custom-call(f32[128,128]{1,0:T(8,128)S(1)} %cholesky.580), custom_call_target="Cholesky" | custom-call | tf_op jit(solution)/shard_map/jit(cholesky)/cholesky | solution.py:32
  553.5 9.8 %custom-call.63 = f32[1,128,128]{1,2,0:T(8,128)S(1)} custom-call(f32[1,128,128]{2,1,0:T(8,128)S(1)} %get-tuple-element.69), custom_call_target="InvertDiagBlocksLowerTriangular" | custom-call | tf_op jit(solution)/shard_map/jit(cholesky)/cholesky | solution.py:32
  567.2 12.1 %cholesky.244 = f32[128,128]{1,0:T(8,128)S(1)} custom-call(f32[128,128]{1,0:T(8,128)S(1)} %cholesky.584), custom_call_target="Cholesky" | custom-call | tf_op jit(solution)/shard_map/jit(cholesky)/cholesky | solution.py:32
  580.0 9.8 %custom-call.64 = f32[1,128,128]{1,2,0:T(8,128)S(1)} custom-call(f32[1,128,128]{2,1,0:T(8,128)S(1)} %get-tuple-element.66), custom_call_target="InvertDiagBlocksLowerTriangular" | custom-call | tf_op jit(solution)/shard_map/jit(cholesky)/cholesky | solution.py:32
  593.1 11.7 %cholesky.468 = f32[128,128]{1,0:T(8,128)S(1)} custom-call(f32[128,128]{1,0:T(8,128)S(1)} %cholesky.589), custom_call_target="Cholesky" | custom-call | tf_op jit(solution)/shard_map/jit(cholesky)/cholesky | solution.py:32
  606.1 9.8 %custom-call.65 = f32[1,128,128]{1,2,0:T(8,128)S(1)} custom-call(f32[1,128,128]{2,1,0:T(8,128)S(1)} %get-tuple-element.63), custom_call_target="InvertDiagBlocksLowerTriangular" | custom-call | tf_op jit(solution)/shard_map/jit(cholesky)/cholesky | solution.py:32
  619.4 11.8 %cholesky.487 = f32[128,128]{1,0:T(8,128)S(1)} custom-call(f32[128,128]{1,0:T(8,128)S(1)} %cholesky.594), custom_call_target="Cholesky" | custom-call | tf_op jit(solution)/shard_map/jit(cholesky)/cholesky | solution.py:32
  632.6 9.8 %custom-call.66 = f32[1,128,128]{1,2,0:T(8,128)S(1)} custom-call(f32[1,128,128]{2,1,0:T(8,128)S(1)} %get-tuple-element.60), custom_call_target="InvertDiagBlocksLowerTriangular" | custom-call | tf_op jit(solution)/shard_map/jit(cholesky)/cholesky | solution.py:32
  645.8 11.7 %cholesky.506 = f32[128,128]{1,0:T(8,128)S(1)} custom-call(f32[128,128]{1,0:T(8,128)S(1)} %cholesky.599), custom_call_target="Cholesky" | custom-call | tf_op jit(solution)/shard_map/jit(cholesky)/cholesky | solution.py:32
  658.8 10.0 %custom-call.67 = f32[1,128,128]{1,2,0:T(8,128)S(1)} custom-call(f32[1,128,128]{2,1,0:T(8,128)S(1)} %get-tuple-element.57), custom_call_target="InvertDiagBlocksLowerTriangular" | custom-call | tf_op jit(solution)/shard_map/jit(cholesky)/cholesky | solution.py:32
  672.1 11.7 %cholesky.526 = f32[128,128]{1,0:T(8,128)S(1)} custom-call(f32[128,128]{1,0:T(8,128)S(1)} %cholesky.604), custom_call_target="Cholesky" | custom-call | tf_op jit(solution)/shard_map/jit(cholesky)/cholesky | solution.py:32
  685.1 9.8 %custom-call.68 = f32[1,128,128]{1,2,0:T(8,128)S(1)} custom-call(f32[1,128,128]{2,1,0:T(8,128)S(1)} %get-tuple-element.54), custom_call_target="InvertDiagBlocksLowerTriangular" | custom-call | tf_op jit(solution)/shard_map/jit(cholesky)/cholesky | solution.py:32
  697.9 12.1 %cholesky.546 = f32[128,128]{1,0:T(8,128)S(1)} custom-call(f32[128,128]{1,0:T(8,128)S(1)} %cholesky.609), custom_call_target="Cholesky" | custom-call | tf_op jit(solution)/shard_map/jit(cholesky)/cholesky | solution.py:32
  711.3 9.8 %custom-call.69 = f32[1,128,128]{1,2,0:T(8,128)S(1)} custom-call(f32[1,128,128]{2,1,0:T(8,128)S(1)} %get-tuple-element.51), custom_call_target="InvertDiagBlocksLowerTriangular" | custom-call | tf_op jit(solution)/shard_map/jit(cholesky)/cholesky | solution.py:32
  723.7 11.7 %cholesky.564 = f32[128,128]{1,0:T(8,128)S(1)} custom-call(f32[128,128]{1,0:T(8,128)S(1)} %convolution_subtract_fusion.13), custom_call_target="Cholesky" | custom-call | tf_op jit(solution)/shard_map/jit(cholesky)/cholesky | solution.py:32
  747.1 22.8 %while.1 = (s32[]{:T(128)}, f32[1024,1024]{1,0:T(8,128)}, s32[8,2]{0,1:T(2,128)S(1)}, f32[8,128,128]{2,1,0:T(8,128)S(1)}, s32[]{:T(128)}) while((s32[]{:T(128)}, f32[1024,1024]{1,0:T(8,128)}, s32[8,2]{0,1:T(2,128)S(1)}, f32[8,128,128]{2,1,0:T(8,128)S(1)}, s32[]{:T(128)}) %tuple.58), condition=%wide.while_cond, body=%wide.while_body.sunk | while | flops 2 | bytes 131181 | solution.py:33
  769.9 78.8 %custom-call.70 = f32[8,128,128]{1,2,0:T(8,128)S(1)} custom-call(f32[8,128,128]{2,1,0:T(8,128)S(1)} %get-tuple-element.12), custom_call_target="InvertDiagBlocksLowerTriangular" | custom-call | tf_op jit(solution)/shard_map/jit(_solve_triangular)/triangular_solve | solution.py:33
  (108 shorter events, 91.4 us)
Async XLA Ops:
  6.5 83.8 %copy-start.1 = (bf16[768,1024]{1,0:T(8,128)(2,1)S(1)}, bf16[768,1024]{1,0:T(8,128)(2,1)}, u32[]{:S(2)}) copy-start(bf16[768,1024]{1,0:T(8,128)(2,1)} %param.8) | copy-start | bytes 4718596
  6.5 83.8 %copy-start.4 = (f32[1024]{0:T(1024)S(1)}, f32[1024]{0:T(1024)}, u32[]{:S(2)}) copy-start(f32[1024]{0:T(1024)} %param.11) | copy-start | bytes 12292
  6.5 83.8 %copy-start.3 = (f32[1024]{0:T(1024)S(1)}, f32[1024]{0:T(1024)}, u32[]{:S(2)}) copy-start(f32[1024]{0:T(1024)} %param.12) | copy-start | bytes 12292
  6.5 83.8 %copy-start.2 = (f32[4096]{0:T(1024)S(1)}, f32[4096]{0:T(1024)}, u32[]{:S(2)}) copy-start(f32[4096]{0:T(1024)} %param.14) | copy-start | bytes 49156
  6.5 83.8 %all-gather.5.cloned.1.call-start = ((), (), s32[]{:S(2)}) async-start(), calls=%async_computation | async-start | bytes 8912896 | tf_op jit(solution)/shard_map/all_gather | solution.py:18
  7.3 158.3 %all-gather.7.cloned.1.call-start = ((), (), s32[]{:S(2)}) async-start(), calls=%async_computation.1 | async-start | bytes 8912896 | tf_op jit(solution)/shard_map/all_gather | solution.py:19
  8.0 496.5 %all-gather.9.cloned.1.call-start = ((), (), s32[]{:S(2)}) async-start(), calls=%async_computation.2 | async-start | bytes 71303168 | tf_op jit(solution)/shard_map/all_gather | solution.py:31
  537.3 1.9 copy-start
Sparse Core Ops, SparseCore 0:
  9.5 80.7 all-gather.4
  92.5 73.0 all-gather.6
  180.1 324.3 all-gather.8
